TPU v7x, 32 devices: a whole 2x2x4 slice. The times are simulated.
32 devices in a mesh: groups: 2 (over x), rows: 16 (over z, y, core).
Axes of the slice: x: 2, y: 2, z: 4, core: 2. Of those that a mesh axis runs over, the one named last changes fastest.
Arguments:
- dictionary: bfloat16 [8192, 32768], P('rows'), may hold values from -0.0625 to 0.0625
- patches: bfloat16 [8192, 2048], P('rows', 'groups'), parts along dimension 1, may hold values from -6 to 6
- initial_codes: bfloat16 [32, 16, 4096], P(('groups', 'rows')), parts along dimension 0, may hold values from -3 to 3
- support: int32 [32, 16], P('groups'), parts along dimension 0, may hold values from 0 to 511, as said below
- counts: int32 [32], P('groups'), parts along dimension 0, may hold values from 4 to 16, as said below
- group_order: int32 [32], P('groups'), parts along dimension 0, may hold values from 0 to 15, each once
- penalty: float32 [32, 64], P('groups'), parts along dimension 0, may hold values from 0.05 to 0.5
Outputs:
- codes: float32 [32, 16, 4096], P(('groups', 'rows')), parts along dimension 0
There are 2 independent parts, one for each index of `groups`. A program takes and returns all parts, laid end to end along the dimension named above; an argument that names none is the same for every part. Nothing has to cross between parts.
Inputs may be any that keep to these rules, and one draw needn't show every extreme that they name: `support`: in each group's list the first counts entries are distinct block ids; entries at positions counts and beyond are padding and are ignored. The counts of one part sum to exactly 160.
All inputs are finite; a program needn't handle non-finite values.
Results may differ from a plain program's by a relative error of at most 0.0055.
Values may be sent and summed in bfloat16 or wider, within the bound.
A program may use at most 192 MiB of HBM per device.

v0:
```python
import jax
import jax.numpy as jnp
from jax import lax
from jax.sharding import PartitionSpec as P

BLOCK = 64
SLOTS = 16
PATCHES = 64
ITERS = 3


def momentum_list():
    values = []
    tvalue = 1.0
    for turn in range(ITERS):
        tnext = (1.0 + (1.0 + 4.0 * tvalue * tvalue) ** 0.5) / 2.0
        values.append((tvalue - 1.0) / tnext)
        tvalue = tnext
    return values


def local(dictionary, patches, initial_codes, support, counts, group_order, penalty):
    pixel_rows = dictionary.shape[0]
    groups = group_order.shape[0]
    nblocks = dictionary.shape[1] // BLOCK
    tile_size = PATCHES * BLOCK
    devices_axis = lax.axis_size("rows")
    position = lax.axis_index("rows")
    owned = groups // devices_axis
    momenta = momentum_list()
    blocks_all = dictionary.reshape(pixel_rows, nblocks, BLOCK)
    ordered_ids = jnp.take(support, group_order, axis=0)
    ordered_counts = jnp.take(counts, group_order, axis=0)
    live_grid = jnp.arange(SLOTS)[None, :] < ordered_counts[:, None]
    targets = jnp.take(patches.reshape(pixel_rows, groups, PATCHES), group_order, axis=1)
    thresh_all = 0.5 * jnp.repeat(jnp.take(penalty, group_order, axis=0), BLOCK, axis=1)
    first_owned = position * owned
    local_live = lax.dynamic_slice_in_dim(live_grid, first_owned, owned, 0)
    masked = initial_codes * local_live[:, :, None].astype(jnp.bfloat16)

    def group_terms(point_full, group_count):
        dict_blocks = jnp.take(blocks_all, ordered_ids, axis=1)
        code_block = point_full
        code_block = code_block.reshape(group_count, SLOTS, PATCHES, BLOCK)
        residual = jnp.einsum(
            "pgsa,gsna->pgn", dict_blocks, code_block, preferred_element_type=jnp.float32
        )
        residual = (residual - targets.astype(jnp.float32)).astype(jnp.bfloat16)
        gradient = jnp.einsum(
            "pgn,pgsa->gsna", residual, dict_blocks, preferred_element_type=jnp.float32
        )
        return gradient.reshape(group_count * SLOTS, tile_size)

    start_full = lax.all_gather(masked, "rows", axis=0, tiled=True)
    live_float = local_live[:, :, None].astype(jnp.float32)
    local_thresh = lax.dynamic_slice_in_dim(thresh_all, first_owned, owned, 0)[:, None, :]
    previous = masked.astype(jnp.float32)
    point_loc = previous
    point_full = start_full
    for turn in range(ITERS):

        def partial_term(row_start, row_count, current_full=point_full):
            return group_terms(current_full, row_count // SLOTS)

        gradient = lax.psum_scatter(
            partial_term(jnp.int32(0), lax.axis_size("rows") * (owned * SLOTS)),
            "rows",
            scatter_dimension=0,
            tiled=True,
        )
        gradient = gradient.reshape(owned, SLOTS, tile_size)
        stepped = point_loc - 0.5 * gradient
        current = (stepped - jnp.clip(stepped, -local_thresh, local_thresh)) * live_float
        point_loc = current + momenta[turn] * (current - previous)
        previous = current
        if turn + 1 < ITERS:
            point_full = lax.all_gather(point_loc.astype(jnp.bfloat16), "rows", axis=0, tiled=True)
    return previous


def solution(mesh):
    in_specs = (
        P("rows", None),
        P("rows", "groups"),
        P(("groups", "rows"), None, None),
        P("groups", None),
        P("groups"),
        P("groups"),
        P("groups", None),
    )
    out_specs = P(("groups", "rows"), None, None)
    return jax.shard_map(local, mesh=mesh, in_specs=in_specs, out_specs=out_specs, check_vma=False)
```

profile of v0, /device:TPU:0, one launch (start us, length us, event | category | flops | bytes accessed | tf_op | source)
XLA Modules:
  0.0 524.2 jit_solution(1216521591889111576)
XLA Ops:
  6.5 0.0 copy-start
  6.5 0.0 all-gather.4.cloned.1.call-start
  6.5 0.7 compare_select_fusion.1
  7.2 1.3 gather_fusion
  8.5 0.7 broadcast_select_fusion.8
  9.2 0.6 dynamic-slice
  9.8 0.6 fusion.48
  10.4 1.6 broadcast_multiply_fusion
  12.1 0.0 all-gather.4.cloned.1.call-update
  12.1 0.0 reduce-scatter.4.cloned.1.call-start
  12.2 1.3 gather_fusion.1
  13.4 0.1 compare_and_fusion
  13.5 0.1 reshape.136
  13.6 0.0 copy-start.4
  13.6 44.1 %copy.14 = bf16[512,32768]{0,1:T(8,128)(2,1)} copy(bf16[512,32768]{1,0:T(8,128)(2,1)} %param.9) | data formatting | bytes 67108864 | tf_op args[0]
  57.7 0.0 copy-done.4
  57.7 0.5 copy.15
  58.2 0.6 gather_fusion.2
  58.9 12.6 %gather_fusion.4 = bf16[256,512,64]{1,2,0:T(8,128)(2,1)} fusion(bf16[512,512,64]{0,2,1:T(8,128)(2,1)} %bitcast.149, s32[1024]{0:T(1024)S(1)} %pad_clamp_fusion), kind=kCustom, calls=%fused_computation.clone | custom fusion | bytes 33555456 | tf_op jit(solution)/shard_map/jit(_take)/gather | solution.py:42
  71.5 0.0 all-gather.4.cloned.1.call-done
  71.5 6.9 %reshape.81 = bf16[16,16,64,64]{3,2,1,0:T(8,128)(2,1)} reshape(bf16[16,16,4096]{2,1,0:T(8,128)(2,1)} %all-gather.4.cloned.1.call-done) | data formatting | bytes 4194304 | tf_op jit(solution)/shard_map/reshape | solution.py:44
  78.4 22.6 %fusion.12 = f32[16,16,64,64]{2,3,1,0:T(8,128)} fusion(bf16[16,16,512,64]{2,3,1,0:T(8,128)(2,1)} %bitcast.150, pred[16,16]{1,0:T(8,128)(4,1)S(1)} %get-tuple-element.10, bf16[16,16,64,64]{3,2,1,0:T(8,128)(2,1)} %reshape.81, bf16[16,512,64]{1,2,0:T(8,128)(2,1)S(1)} %gather_fusion.2, pred[16]{0:T(512)(128)(4,1)S(1)} %get-tuple-element.9), kind=kOutput, calls=%fused_computation.18 | convolution fusion | flops 2166358016 | bytes 24117520 | tf_op jit(solution)/shard_map/pgn,pgsa->gsna/dot_general | solution.py:49
  101.0 9.2 %copy.16 = f32[16,16,64,64]{3,2,1,0:T(8,128)} copy(f32[16,16,64,64]{2,3,1,0:T(8,128)} %fusion.12) | data formatting | bytes 8388608 | tf_op jit(solution)/shard_map/pgn,pgsa->gsna/transpose | solution.py:49
  110.3 0.0 copy-start.2
  110.3 8.0 %reshape.83 = f32[256,4096]{1,0:T(8,128)} reshape(f32[16,16,64,64]{3,2,1,0:T(8,128)} %copy.16) | data formatting | bytes 8388608 | tf_op jit(solution)/shard_map/reshape | solution.py:52
  118.2 0.0 reduce-scatter.4.cloned.1.call-update
  118.2 0.0 all-gather.6.cloned.1.call-start
  118.3 0.0 copy-done
  118.3 0.6 gather_fusion.3
  118.9 0.1 select_multiply_fusion
  118.9 0.2 broadcast_in_dim.58
  119.1 0.2 mul.71
  119.4 0.6 fusion.49
  120.0 73.5 %reduce-scatter.4.cloned.1.call-done = f32[16,4096]{1,0:T(8,128)} async-done(((f32[256,4096]{1,0:T(8,128)}), f32[16,4096]{1,0:T(8,128)}) %reduce-scatter.4.cloned.1.call-update) | async-done | bytes 262160 | tf_op jit(solution)/shard_map/reduce_scatter | solution.py:65
  193.5 0.0 copy-done.2
  193.5 1.8 fusion.47
  195.3 0.0 all-gather.6.cloned.1.call-update
  195.3 0.2 reduce-scatter.6.cloned.1.call-start
  195.5 40.7 %all-gather.6.cloned.1.call-done = bf16[16,16,4096]{2,1,0:T(8,128)(2,1)} async-done(((bf16[1,16,4096]{2,1,0:T(8,128)(2,1)}), bf16[16,16,4096]{2,1,0:T(8,128)(2,1)}) %all-gather.6.cloned.1.call-update) | async-done | bytes 2097168 | tf_op jit(solution)/shard_map/all_gather | solution.py:77
  236.2 6.9 %reshape.84 = bf16[16,16,64,64]{3,2,1,0:T(8,128)(2,1)} reshape(bf16[16,16,4096]{2,1,0:T(8,128)(2,1)} %all-gather.6.cloned.1.call-done) | data formatting | bytes 4194304 | tf_op jit(solution)/shard_map/reshape | solution.py:44
  243.1 22.6 %fusion.15 = f32[16,16,64,64]{2,3,1,0:T(8,128)} fusion(bf16[16,16,512,64]{2,3,1,0:T(8,128)(2,1)} %bitcast.151, pred[16,16]{1,0:T(8,128)(4,1)S(1)} %get-tuple-element.10, bf16[16,16,64,64]{3,2,1,0:T(8,128)(2,1)} %reshape.84, bf16[16,512,64]{1,2,0:T(8,128)(2,1)S(1)} %gather_fusion.2, pred[16]{0:T(512)(128)(4,1)S(1)} %get-tuple-element.9), kind=kOutput, calls=%fused_computation.19 | convolution fusion | flops 2166358016 | bytes 24117520 | tf_op jit(solution)/shard_map/pgn,pgsa->gsna/dot_general | solution.py:49
  265.8 9.2 %copy.17 = f32[16,16,64,64]{3,2,1,0:T(8,128)} copy(f32[16,16,64,64]{2,3,1,0:T(8,128)} %fusion.15) | data formatting | bytes 8388608 | tf_op jit(solution)/shard_map/pgn,pgsa->gsna/transpose | solution.py:49
  275.0 0.0 copy-start.3
  275.0 8.0 %reshape.85 = f32[256,4096]{1,0:T(8,128)} reshape(f32[16,16,64,64]{3,2,1,0:T(8,128)} %copy.17) | data formatting | bytes 8388608 | tf_op jit(solution)/shard_map/reshape | solution.py:52
  283.0 0.0 reduce-scatter.6.cloned.1.call-update
  283.0 0.0 all-gather.8.cloned.1.call-start
  283.1 71.6 %reduce-scatter.6.cloned.1.call-done = f32[16,4096]{1,0:T(8,128)} async-done(((f32[256,4096]{1,0:T(8,128)}), f32[16,4096]{1,0:T(8,128)}) %reduce-scatter.6.cloned.1.call-update) | async-done | bytes 262160 | tf_op jit(solution)/shard_map/reduce_scatter | solution.py:65
  354.7 0.0 copy-done.3
  354.7 1.9 fusion.56
  356.5 0.0 all-gather.8.cloned.1.call-update
  356.5 0.0 reduce-scatter.8.cloned.1.call-start
  356.6 40.6 %all-gather.8.cloned.1.call-done = bf16[16,16,4096]{2,1,0:T(8,128)(2,1)} async-done(((bf16[1,16,4096]{2,1,0:T(8,128)(2,1)}), bf16[16,16,4096]{2,1,0:T(8,128)(2,1)}) %all-gather.8.cloned.1.call-update) | async-done | bytes 2097168 | tf_op jit(solution)/shard_map/all_gather | solution.py:77
  397.2 6.9 %reshape.86 = bf16[16,16,64,64]{3,2,1,0:T(8,128)(2,1)} reshape(bf16[16,16,4096]{2,1,0:T(8,128)(2,1)} %all-gather.8.cloned.1.call-done) | data formatting | bytes 4194304 | tf_op jit(solution)/shard_map/reshape | solution.py:44
  404.1 22.6 %fusion.18 = f32[16,16,64,64]{2,3,1,0:T(8,128)} fusion(bf16[16,16,512,64]{2,3,1,0:T(8,128)(2,1)} %bitcast.152, pred[16,16]{1,0:T(8,128)(4,1)S(1)} %get-tuple-element.10, bf16[16,16,64,64]{3,2,1,0:T(8,128)(2,1)} %reshape.86, bf16[16,512,64]{1,2,0:T(8,128)(2,1)S(1)} %gather_fusion.2, pred[16]{0:T(512)(128)(4,1)S(1)} %get-tuple-element.9), kind=kOutput, calls=%fused_computation.20 | convolution fusion | flops 2166358016 | bytes 24117520 | tf_op jit(solution)/shard_map/pgn,pgsa->gsna/dot_general | solution.py:49
  426.7 0.0 copy-start.1
  426.7 9.3 %copy.18 = f32[16,16,64,64]{3,2,1,0:T(8,128)} copy(f32[16,16,64,64]{2,3,1,0:T(8,128)} %fusion.18) | data formatting | bytes 8388608 | tf_op jit(solution)/shard_map/pgn,pgsa->gsna/transpose | solution.py:49
  436.0 7.9 %reshape.87 = f32[256,4096]{1,0:T(8,128)} reshape(f32[16,16,64,64]{3,2,1,0:T(8,128)} %copy.18) | data formatting | bytes 8388608 | tf_op jit(solution)/shard_map/reshape | solution.py:52
  443.9 0.0 reduce-scatter.8.cloned.1.call-update
  443.9 71.7 %reduce-scatter.8.cloned.1.call-done = f32[16,4096]{1,0:T(8,128)} async-done(((f32[256,4096]{1,0:T(8,128)}), f32[16,4096]{1,0:T(8,128)}) %reduce-scatter.8.cloned.1.call-update) | async-done | bytes 262160 | tf_op jit(solution)/shard_map/reduce_scatter | solution.py:65
  515.6 1.7 subtract_multiply_fusion
  517.4 0.0 copy-done.1
  (4 shorter events, 0.0 us)
Async XLA Ops:
  6.5 111.8 %copy-start = (f32[16,64]{1,0:T(8,128)S(1)}, f32[16,64]{1,0:T(8,128)}, u32[]{:S(2)}) copy-start(f32[16,64]{1,0:T(8,128)} %param.15) | copy-start | bytes 12292
  6.5 64.9 %all-gather.4.cloned.1.call-start = ((), (), s32[]{:S(2)}) async-start(), calls=%async_computation.3 | async-start | bytes 2228224 | tf_op jit(solution)/shard_map/all_gather | solution.py:54
  12.1 181.4 %reduce-scatter.4.cloned.1.call-start = ((), (), s32[]{:S(2)}) async-start(), calls=%async_computation.4 | async-start | bytes 4456448 | tf_op jit(solution)/shard_map/reduce_scatter | solution.py:65
  13.6 44.1 %copy-start.4 = (bf16[512,1024]{1,0:T(8,128)(2,1)S(1)}, bf16[512,1024]{1,0:T(8,128)(2,1)}, u32[]{:S(2)}) copy-start(bf16[512,1024]{1,0:T(8,128)(2,1)} %param.10) | copy-start | bytes 3145732
  110.3 83.2 %copy-start.2 = (bf16[1,16,4096]{2,1,0:T(8,128)(2,1)S(1)}, bf16[1,16,4096]{2,1,0:T(8,128)(2,1)}, u32[]{:S(2)}) copy-start(bf16[1,16,4096]{2,1,0:T(8,128)(2,1)} %param.11) | copy-start | bytes 393220
  118.2 118.0 %all-gather.6.cloned.1.call-start = ((), (), s32[]{:S(2)}) async-start(), calls=%async_computation.5 | async-start | bytes 2228224 | tf_op jit(solution)/shard_map/all_gather | solution.py:77
  195.3 159.4 %reduce-scatter.6.cloned.1.call-start = ((), (), s32[]{:S(2)}) async-start(), calls=%async_computation.6 | async-start | bytes 4456448 | tf_op jit(solution)/shard_map/reduce_scatter | solution.py:65
  275.0 79.7 %copy-start.3 = (f32[16,4096]{1,0:T(8,128)S(1)}, f32[16,4096]{1,0:T(8,128)}, u32[]{:S(2)}) copy-start(f32[16,4096]{1,0:T(8,128)} %reduce-scatter.4.cloned.1.call-done) | copy-start | bytes 786436
  283.0 114.2 %all-gather.8.cloned.1.call-start = ((), (), s32[]{:S(2)}) async-start(), calls=%async_computation.7 | async-start | bytes 2228224 | tf_op jit(solution)/shard_map/all_gather | solution.py:77
  356.5 159.1 %reduce-scatter.8.cloned.1.call-start = ((), (), s32[]{:S(2)}) async-start(), calls=%async_computation.8 | async-start | bytes 4456448 | tf_op jit(solution)/shard_map/reduce_scatter | solution.py:65
  426.7 90.6 %copy-start.1 = (f32[16,64]{1,0:T(8,128)S(1)}, f32[16,64]{1,0:T(8,128)}, u32[]{:S(2)}) copy-start(f32[16,64]{1,0:T(8,128)} %param.15) | copy-start | bytes 12292
Sparse Core Ops, SparseCore 0:
  12.2 44.1 all-gather.3
  118.4 75.0 reduce-scatter.3
  195.7 40.5 all-gather.5
  283.1 71.4 reduce-scatter.5
  356.7 40.4 all-gather.7
  444.1 71.5 reduce-scatter.7
where the time goes:
time: 527 us; the launch traced here: 524 us
  waiting for transfers between devices  298 us (57%)
  local copies, waits for them, and re-layouts  134 us (25%)
  matrix products  67.9 us (13%)
  between operations  13.6 us (3%)
  other arithmetic  9.8 us (2%)
    reduce_scatter x3, waiting for transfers between devices, local(): lax.psum_scatter(partial_term(jnp.int32(0), lax.axis_size('rows') * (owne...  217 us
    all_gather x2, waiting for transfers between devices, local(): lax.all_gather(point_loc.astype(jnp.bfloat16), 'rows', axis=0, tiled=True)  81.3 us
    dot_general x3, matrix products, group_terms(): jnp.einsum('pgn,pgsa->gsna', residual, dict_blocks, preferred_element_typ...  67.9 us
    unnamed x12, local copies, waits for them, and re-layouts  44.7 us
    transpose x3, local copies, waits for them, and re-layouts, group_terms(): jnp.einsum('pgn,pgsa->gsna', residual, dict_blocks, preferred_element_typ...  27.7 us
    reshape x3, local copies, waits for them, and re-layouts, group_terms(): return gradient.reshape(group_count * SLOTS, tile_size)  23.9 us
    reshape x3, local copies, waits for them, and re-layouts, group_terms(): code_block = code_block.reshape(group_count, SLOTS, PATCHES, BLOCK)  20.7 us
    gather x1, local copies, waits for them, and re-layouts, group_terms(): dict_blocks = jnp.take(blocks_all, ordered_ids, axis=1)  12.6 us
  transfers between devices with their start and end apart: 6, of which 5 were waited for; matrix products, arithmetic and copies ran while one was open for 12% of the time, Pallas kernels for 0%

commit v1 on v0

v1 whole, which is shorter than its diff:
```python
import functools

import jax
import jax.numpy as jnp
from jax import lax
from jax.experimental import pallas as pl
from jax.experimental.pallas import tpu as pltpu
from jax.sharding import PartitionSpec as P

BLOCK = 64
SLOTS = 16
PATCHES = 64
ITERS = 3
LIVE = 10
PER_STEP = 8
F32 = jnp.float32
BF16 = jnp.bfloat16
VMEM = pltpu.VMEM


def momentum_list():
    values = []
    tvalue = 1.0
    for turn in range(ITERS):
        tnext = (1.0 + (1.0 + 4.0 * tvalue * tvalue) ** 0.5) / 2.0
        values.append((tvalue - 1.0) / tnext)
        tvalue = tnext
    return values


def gather_kernel(ids_ref, *refs):
    out_ref = refs[-1]
    step = pl.program_id(0)
    lane = lax.broadcasted_iota(jnp.int32, (out_ref.shape[1], 128), 1)
    for pair in range(PER_STEP // 2):
        sides = []
        for side in range(2):
            slot = 2 * pair + side
            half = ids_ref[step * PER_STEP + slot] % 2
            tile = refs[slot][...].astype(F32)
            turned = pltpu.roll(tile, 64, 1)
            sides.append(jnp.where(half == side, tile, turned))
        both = jnp.where(lane < 64, sides[0], sides[1]).astype(BF16)
        out_ref[pair // 2, :, pl.ds((pair % 2) * 128, 128)] = both


def gather_blocks(dictionary, ids):
    rows = dictionary.shape[0]
    entries = ids.shape[0]

    def spec(slot):
        return pl.BlockSpec((rows, 128), lambda i, ids_ref: (0, ids_ref[i * PER_STEP + slot] // 2))

    return pl.pallas_call(
        gather_kernel,
        out_shape=jax.ShapeDtypeStruct((entries // 4, rows, 256), BF16),
        grid_spec=pltpu.PrefetchScalarGridSpec(
            num_scalar_prefetch=1,
            grid=(entries // PER_STEP,),
            in_specs=[spec(slot) for slot in range(PER_STEP)],
            out_specs=pl.BlockSpec((PER_STEP // 4, rows, 256), lambda i, ids_ref: (i, 0, 0)),
        ),
        name="gather_blocks",
    )(ids, *([dictionary] * PER_STEP))


def share_kernel(first_ref, last_ref, split_ref, s_ref, z_ref, y_ref, out_ref, r_ref, rb_ref):
    quads = s_ref.shape[0]
    lane = lax.broadcasted_iota(jnp.int32, (PATCHES, 256), 1) // BLOCK
    r_ref[...] = -y_ref[...].astype(F32)

    def forward(quad, carry):
        z = jnp.concatenate([z_ref[2 * quad], z_ref[2 * quad + 1]], axis=1).astype(F32)
        mask = lane < split_ref[quad]
        zz = jnp.concatenate([jnp.where(mask, z, 0.0), jnp.where(mask, 0.0, z)], axis=0).astype(BF16)
        term = lax.dot_general(zz, s_ref[quad], (((1,), (1,)), ((), ())), preferred_element_type=F32)
        r_ref[first_ref[quad]] += term[:PATCHES]
        r_ref[last_ref[quad]] += term[PATCHES:]
        return carry

    lax.fori_loop(0, quads, forward, 0, unroll=2)
    rb_ref[...] = r_ref[...].astype(BF16)

    def backward(quad, carry):
        rr = jnp.concatenate([rb_ref[first_ref[quad]], rb_ref[last_ref[quad]]], axis=0)
        gr = jnp.dot(rr, s_ref[quad], preferred_element_type=F32)
        g = jnp.where(lane < split_ref[quad], gr[:PATCHES], gr[PATCHES:]).astype(BF16)
        out_ref[2 * quad] = g[:, :128]
        out_ref[2 * quad + 1] = g[:, 128:]
        return carry

    lax.fori_loop(0, quads, backward, 0, unroll=2)


def gradient_share(first, last, split, blocks, z, targets):
    groups, patches, rows = targets.shape
    smem = pl.BlockSpec(memory_space=pltpu.SMEM)
    vmem = pl.BlockSpec(memory_space=VMEM)
    return pl.pallas_call(
        share_kernel,
        out_shape=jax.ShapeDtypeStruct(z.shape, BF16),
        in_specs=[smem, smem, smem, vmem, vmem, vmem],
        out_specs=vmem,
        scratch_shapes=[VMEM((groups, patches, rows), F32), VMEM((groups, patches, rows), BF16)],
        compiler_params=pltpu.CompilerParams(vmem_limit_bytes=40 * 1024 * 1024),
        name="gradient_share",
    )(first, last, split, blocks, z, targets)


class Place:
    def __init__(self, devices):
        self.me = lax.axis_index("rows")
        self.fars = devices // 4
        self.core = self.me % 2
        self.near = (self.me // 2) % 2
        self.far = self.me // 4

    def index(self, far, near, core):
        return (far * 2 + near) * 2 + core

    def far_at(self, distance):
        return (self.far + distance) % self.fars

    def far_before(self, distance):
        return (self.far + self.fars - distance) % self.fars

    def far_peer(self, distance):
        return self.index(self.far_at(distance), self.near, self.core)

    def near_peer(self):
        return self.index(self.far, 1 - self.near, self.core)

    def core_peer(self):
        return self.index(self.far, self.near, 1 - self.core)


def send(src, dst, send_sem, recv_sem, peer):
    copy = pltpu.make_async_remote_copy(
        src_ref=src,
        dst_ref=dst,
        send_sem=send_sem,
        recv_sem=recv_sem,
        device_id=(lax.axis_index("groups"), peer),
        device_id_type=pl.DeviceIdType.MESH,
    )
    copy.start()
    return copy


def greet(at):
    barrier = pltpu.get_barrier_semaphore()
    peers = [at.core_peer(), at.near_peer()] + [at.far_peer(d) for d in range(1, at.fars)]
    for peer in peers:
        pl.semaphore_signal(
            barrier, inc=1, device_id=(lax.axis_index("groups"), peer), device_id_type=pl.DeviceIdType.MESH
        )
    pl.semaphore_wait(barrier, len(peers))


def spread(at, all_ref, sems):
    far_s, far_r, near_s, near_r, core_s, core_r = sems
    mine = all_ref.at[at.me]
    far_copies = [
        send(mine, mine, far_s.at[d - 1], far_r.at[d - 1], at.far_peer(d)) for d in range(1, at.fars)
    ]
    near_copies = [send(mine, mine, near_s.at[0], near_r.at[0], at.near_peer())]
    core_copies = [send(mine, mine, core_s.at[0], core_r.at[0], at.core_peer())]
    slot = 1
    for d in range(at.fars):
        if d:
            far_copies[d - 1].wait_recv()
            came = all_ref.at[at.index(at.far_before(d), at.near, at.core)]
            near_copies.append(send(came, came, near_s.at[d], near_r.at[d], at.near_peer()))
            core_copies.append(send(came, came, core_s.at[slot], core_r.at[slot], at.core_peer()))
            slot += 1
        if d:
            near_copies[d - 1].wait_recv()
            came = all_ref.at[at.index(at.far_before(d - 1), 1 - at.near, at.core)]
            core_copies.append(send(came, came, core_s.at[slot], core_r.at[slot], at.core_peer()))
            slot += 1
    last = at.fars - 1
    near_copies[last].wait_recv()
    came = all_ref.at[at.index(at.far_before(last), 1 - at.near, at.core)]
    core_copies.append(send(came, came, core_s.at[slot], core_r.at[slot], at.core_peer()))
    for copy in core_copies:
        copy.wait_recv()
    for copy in far_copies + near_copies + core_copies:
        copy.wait_send()


def gather_codes_kernel(devices, mine_ref, all_ref, own_sem, *sems):
    at = Place(devices)
    own = pltpu.make_async_copy(mine_ref, all_ref.at[at.me], own_sem)
    own.start()
    greet(at)
    own.wait()
    spread(at, all_ref, sems)


def spread_sems(devices):
    fars = devices // 4
    dma = pltpu.SemaphoreType.DMA
    return [dma((fars - 1,)), dma((fars - 1,)), dma((fars,)), dma((fars,)), dma((2 * fars,)), dma((2 * fars,))]


def gather_codes(devices, mine):
    vmem = pl.BlockSpec(memory_space=VMEM)
    return pl.pallas_call(
        functools.partial(gather_codes_kernel, devices),
        out_shape=jax.ShapeDtypeStruct((devices,) + mine.shape, BF16),
        in_specs=[vmem],
        out_specs=vmem,
        scratch_shapes=[pltpu.SemaphoreType.DMA] + spread_sems(devices),
        compiler_params=pltpu.CompilerParams(collective_id=0, has_side_effects=True),
        name="gather_codes",
    )(mine)


def step_kernel(
    devices, weight, share_ref, point_ref, prev_ref, thr_ref, all_ref, newpoint_ref, newprev_ref,
    got_core, got_near, got_far, sum_core, sum_near, kept,
    c_s, c_r, n_s, n_r, f_s, f_r, *sems,
):
    at = Place(devices)
    fars = at.fars
    greet(at)
    order = list(range(1, fars)) + [0]
    core_copies = {}
    for flip in (1, 0):
        for d in order:
            near = at.near if flip == 0 else 1 - at.near
            chunk = share_ref.at[at.index(at.far_at(d), near, 1 - at.core)]
            slot = flip * fars + d
            core_copies[flip, d] = send(chunk, got_core.at[slot], c_s.at[slot], c_r.at[slot], at.core_peer())
    near_copies = {}
    for d in order:
        core_copies[1, d].wait_recv()
        own = share_ref[at.index(at.far_at(d), 1 - at.near, at.core)].astype(F32)
        sum_core[d] = (own + got_core[fars + d].astype(F32)).astype(BF16)
        near_copies[d] = send(sum_core.at[d], got_near.at[d], n_s.at[d], n_r.at[d], at.near_peer())
    far_copies = {}
    for d in order:
        core_copies[0, d].wait_recv()
        own = share_ref[at.index(at.far_at(d), at.near, at.core)].astype(F32)
        total = own + got_core[d].astype(F32)
        near_copies[d].wait_recv()
        total = total + got_near[d].astype(F32)
        if d:
            sum_near[d - 1] = total.astype(BF16)
            far_copies[d] = send(sum_near.at[d - 1], got_far.at[d - 1], f_s.at[d - 1], f_r.at[d - 1], at.far_peer(d))
        else:
            kept[...] = total
    for d in range(1, fars):
        far_copies[d].wait_recv()
        kept[...] += got_far[d - 1].astype(F32)
    stepped = point_ref[...] - 0.5 * kept[...]
    thr = thr_ref[...]
    current = stepped - jnp.clip(stepped, -thr, thr)
    newprev_ref[...] = current
    point = current if weight is None else current + weight * (current - prev_ref[...])
    newpoint_ref[...] = point
    all_ref[at.me] = point.astype(BF16)
    for copy in list(core_copies.values()) + list(near_copies.values()) + list(far_copies.values()):
        copy.wait_send()
    spread(at, all_ref, sems)


def code_step(devices, turn, weight, share, point, prev, thr):
    fars = devices // 4
    chunk = point.shape
    dma = pltpu.SemaphoreType.DMA
    vmem = pl.BlockSpec(memory_space=VMEM)
    return pl.pallas_call(
        functools.partial(step_kernel, devices, weight),
        out_shape=(
            jax.ShapeDtypeStruct(share.shape, BF16),
            jax.ShapeDtypeStruct(chunk, F32),
            jax.ShapeDtypeStruct(chunk, F32),
        ),
        in_specs=[vmem] * 4,
        out_specs=(vmem, vmem, vmem),
        scratch_shapes=[
            VMEM((2 * fars,) + chunk, BF16),
            VMEM((fars,) + chunk, BF16),
            VMEM((fars - 1,) + chunk, BF16),
            VMEM((fars,) + chunk, BF16),
            VMEM((fars - 1,) + chunk, BF16),
            VMEM(chunk, F32),
            dma((2 * fars,)), dma((2 * fars,)), dma((fars,)), dma((fars,)), dma((fars - 1,)), dma((fars - 1,)),
        ]
        + spread_sems(devices),
        compiler_params=pltpu.CompilerParams(
            collective_id=1 + turn, has_side_effects=True, vmem_limit_bytes=40 * 1024 * 1024
        ),
        name="code_step%d" % turn,
    )(share, point, prev, thr)


def local(dictionary, patches, initial_codes, support, counts, group_order, penalty):
    rows = dictionary.shape[0]
    groups = group_order.shape[0]
    devices = lax.axis_size("rows")
    me = lax.axis_index("rows")
    entries = LIVE * groups
    pairs = entries // 2
    chunk_pairs = pairs // devices
    chunk_rows = chunk_pairs * PATCHES

    mine = initial_codes.reshape(SLOTS // 2, 2, PATCHES, BLOCK).transpose(0, 2, 1, 3)
    mine = mine.reshape(SLOTS // 2 * PATCHES, 2 * BLOCK)
    start_all = gather_codes(devices, mine).reshape(groups * SLOTS // 2, PATCHES, 2 * BLOCK)

    ends = jnp.cumsum(counts)
    starts = ends - counts
    entry = jnp.arange(entries, dtype=jnp.int32)
    group_of = jnp.sum((entry[:, None] >= ends[None, :]).astype(jnp.int32), axis=1)
    slot_of = entry - jnp.take(starts, group_of)
    ids = jnp.take(support.reshape(-1), group_of * SLOTS + slot_of)
    quads = group_of.reshape(-1, 4)
    first, last = quads[:, 0], quads[:, 3]
    split = jnp.sum((quads == first[:, None]).astype(jnp.int32), axis=1)
    seat = jnp.argmax(group_order[None, :] == group_of[:, None], axis=1).astype(jnp.int32)

    blocks = gather_blocks(dictionary, ids)
    targets = patches.T.reshape(groups, PATCHES, rows)

    source = (seat * (SLOTS // 2) + slot_of // 2).reshape(pairs, 2)
    half = (slot_of % 2).reshape(pairs, 2)[:, :, None, None] == 0

    def side(which):
        both = jnp.take(start_all, source[:, which], axis=0)
        return jnp.where(half[:, which], both[..., :BLOCK], both[..., BLOCK:])

    z_all = jnp.concatenate([side(0), side(1)], axis=2)
    thr_all = 0.5 * jnp.take(penalty, group_of, axis=0)
    own_thr = lax.dynamic_slice_in_dim(thr_all.reshape(pairs, 2, PATCHES), me * chunk_pairs, chunk_pairs, 0)
    thr = jnp.repeat(own_thr.transpose(0, 2, 1).reshape(chunk_rows, 2), BLOCK, axis=1)
    point = lax.dynamic_slice_in_dim(z_all, me * chunk_pairs, chunk_pairs, 0)
    point = point.reshape(chunk_rows, 2 * BLOCK).astype(F32)
    prev = point
    momenta = momentum_list()
    for turn in range(ITERS):
        share = gradient_share(first, last, split, blocks, z_all, targets)
        weight = momenta[turn] if turn + 1 < ITERS else None
        share = share.reshape(devices, chunk_rows, 2 * BLOCK)
        z_all, point, prev = code_step(devices, turn, weight, share, point, prev, thr)
        z_all = z_all.reshape(pairs, PATCHES, 2 * BLOCK)

    group = lax.dynamic_index_in_dim(group_order, me, 0, keepdims=False)
    begin = jnp.take(starts, group)
    live = jnp.take(counts, group)
    wanted = begin // 2 + jnp.arange(SLOTS // 2 + 1, dtype=jnp.int32)
    near = jnp.take(z_all, jnp.minimum(wanted, pairs - 1), axis=0).astype(F32)
    near = near.reshape(SLOTS // 2 + 1, PATCHES, 2, BLOCK).transpose(0, 2, 1, 3)
    near = near.reshape(SLOTS + 2, PATCHES, BLOCK)
    codes = lax.dynamic_slice_in_dim(near, begin % 2, SLOTS, 0)
    codes = jnp.where((jnp.arange(SLOTS) < live)[:, None, None], codes, 0.0)
    return codes.reshape(1, SLOTS, PATCHES * BLOCK)


def solution(mesh):
    in_specs = (
        P("rows", None),
        P("rows", "groups"),
        P(("groups", "rows"), None, None),
        P("groups", None),
        P("groups"),
        P("groups"),
        P("groups", None),
    )
    out_specs = P(("groups", "rows"), None, None)
    return jax.shard_map(local, mesh=mesh, in_specs=in_specs, out_specs=out_specs, check_vma=False)
```

time: 527 us -> 227 us (0.43)
  waiting for transfers between devices: 298 us -> 0 us
  Pallas kernels: 0 us -> 178 us
  local copies, waits for them, and re-layouts: 134 us -> 25.6 us
  matrix products: 67.9 us -> 0 us
  between operations: 13.6 us -> 3.65 us
  other arithmetic: 9.8 us -> 17.9 us
    reduce_scatter x3 -> x0, waiting for transfers between devices: 217 us -> none  [local(): lax.psum_scatter(partial_term(jnp.int32(0), lax.axis_size('rows') * (owne...]
    pallas_call x0 -> x8, Pallas kernels: none -> 178 us  [the longest x3 95.7 us: code_step(): pl.pallas_call(functools.partial(step_kernel, devices, weight), out_shape...]
    all_gather x3 -> x0, waiting for transfers between devices: 81.3 us -> none  [the longest x2 81.3 us: local(): lax.all_gather(point_loc.astype(jnp.bfloat16), 'rows', axis=0, tiled=True)]
    dot_general x3 -> x0, matrix products: 67.9 us -> none  [group_terms(): jnp.einsum('pgn,pgsa->gsna', residual, dict_blocks, preferred_element_typ...]
    reshape x6 -> x9, local copies, waits for them, and re-layouts: 44.6 us -> 3.41 us  [the longest x1 0.89 us: local(): return codes.reshape(1, SLOTS, PATCHES * BLOCK)]
    unnamed x12 -> x22, local copies, waits for them, and re-layouts: 44.7 us -> 7.36 us
    transpose x3 -> x1, local copies, waits for them, and re-layouts: 27.7 us -> 1.31 us  [local(): targets = patches.T.reshape(groups, PATCHES, rows)]
    add x0 -> x1, other arithmetic: none -> 9.94 us  [local(): source = (seat * (SLOTS // 2) + slot_of // 2).reshape(pairs, 2)]
  transfers between devices with their start and end apart: 6 -> 0, of which waited for: 5 -> 0; matrix products, arithmetic and copies ran while one was open for 12% -> 0% of each run, Pallas kernels for 0% -> 0%
where the time goes in v1:
time: 227 us; the launch traced here: 225 us
  Pallas kernels  178 us (78%)
  local copies, waits for them, and re-layouts  25.6 us (11%)
  other arithmetic  17.9 us (8%)
  between operations  3.65 us (2%)
    pallas_call x3, Pallas kernels, code_step(): pl.pallas_call(functools.partial(step_kernel, devices, weight), out_shape...  95.7 us
    pallas_call x3, Pallas kernels, gradient_share(): pl.pallas_call(share_kernel, out_shape=jax.ShapeDtypeStruct(z.shape, BF16...  35.1 us
    pallas_call x1, Pallas kernels, gather_codes(): pl.pallas_call(functools.partial(gather_codes_kernel, devices), out_shape...  25.9 us
    pallas_call x1, Pallas kernels, gather_blocks(): pl.pallas_call(gather_kernel, out_shape=jax.ShapeDtypeStruct((entries //...  21.4 us
    add x1, other arithmetic, local(): source = (seat * (SLOTS // 2) + slot_of // 2).reshape(pairs, 2)  9.94 us
    unnamed x22, local copies, waits for them, and re-layouts  7.36 us
    gather x2, local copies, waits for them, and re-layouts, side(): both = jnp.take(start_all, source[:, which], axis=0)  5.44 us

profile of v1, /device:TPU:0, one launch (start us, length us, event | category | flops | bytes accessed | tf_op | source)
XLA Modules:
  0.0 225.3 jit_solution(7814725270621205393)
XLA Ops:
  0.0 0.0 copy-start
  0.0 1.2 dynamic_slice.13
  3.2 1.2 dynamic-slice.4
  5.1 0.8 reshape.297
  5.9 0.7 copy.27
  6.7 0.1 reduce.18
  6.8 0.7 sub.37
  7.4 0.1 convert_reduce_fusion.1
  7.5 1.3 iota_reduce_fusion
  8.8 0.7 fusion.10
  10.2 9.9 %fusion.7 = (s32[160]{0:T(256)S(1)}, s32[160]{0:T(256)S(1)}) fusion(s32[160]{0:T(256)S(1)} %get-tuple-element.14, s32[160]{0:T(256)S(1)} %convert_reduce_fusion.1, s32[]{:T(128)} %bitcast.22, s32[]{:T(128)} %bitcast.21, s32[160]{0:T(256)S(1)} %bitcast.69, s32[]{:T(128)} %bitcast.20, s32[]{:T(128)} %bitcast.19, s32[]{:T(128)} %bitcast.18, s32[]{:T(128)} %bitcast.17, ...), kind=kLoop, calls=%fused_computation.81 | loop fusion | flops 8800 | bytes 3264 | tf_op jit(solution)/shard_map/add | solution.py:327
  20.2 0.0 copy-start.10
  20.2 1.6 gather_fusion
  21.8 0.6 and_select_fusion.2.ids_ref
  22.4 0.1 reshape.296
  22.5 0.2 slice_reduce_fusion.4
  22.7 0.2 convert_reduce_fusion.split_ref
  22.9 0.1 gather.37
  23.1 0.1 reshape.301
  23.2 0.2 slice_reduce_fusion.1
  23.4 0.1 reduce_sum.27
  23.6 0.2 slice_reduce_fusion.3
  23.8 0.1 reduce_sum.28
  24.0 0.1 copy.30
  24.1 0.1 constant_dynamic-slice_fusion.1
  24.1 0.0 copy-done
  24.2 0.7 gather_fusion.1
  24.9 0.1 fusion.4
  24.9 0.1 reshape.304
  25.0 0.1 copy.32.thr_ref
  25.1 0.0 copy-done.10
  25.2 0.2 reshape.298
  25.4 0.3 copy.42
  25.7 0.8 reshape.299.mine_ref
  26.5 0.0 copy-done.9
  26.5 1.3 copy.29
  27.8 25.9 %gather_codes.1 = bf16[16,512,128]{2,1,0:T(8,128)(2,1)} custom-call(bf16[512,128]{1,0:T(8,128)(2,1)} %reshape.299.mine_ref), custom_call_target="tpu_custom_call" | custom-call | tf_op jit(solution)/shard_map/gather_codes/pallas_call | solution.py:208
  53.7 0.0 copy-start.7
  53.7 3.6 %gather_fusion.4 = bf16[80,64,128]{2,1,0:T(8,128)(2,1)} fusion(bf16[128,64,128]{2,1,0:T(8,128)(2,1)} %bitcast.58, s32[1024]{0:T(1024)S(1)} %pad_clamp_fusion.2), kind=kCustom, calls=%fused_computation.1.clone | custom fusion | bytes 2621760 | tf_op jit(solution)/shard_map/jit(_take)/gather | solution.py:331
  57.3 1.9 gather_fusion.3
  59.1 1.5 broadcast_select_fusion.1
  60.6 0.5 slice_select_fusion.1
  61.1 0.8 copy-done.8
  61.9 0.2 broadcast_select_fusion
  62.1 0.5 slice_select_fusion
  62.6 0.1 fusion
  62.8 1.8 pad_maximum_fusion.z_ref
  64.6 21.4 %gather_blocks.1.s_ref = bf16[40,512,256]{2,1,0:T(8,128)(2,1)} custom-call(s32[160]{0:T(256)} %and_select_fusion.2.ids_ref, bf16[512,32768]{1,0:T(8,128)(2,1)} %refs_7_.1, bf16[512,32768]{1,0:T(8,128)(2,1)} %refs_7_.1, bf16[512,32768]{1,0:T(8,128)(2,1)} %refs_7_.1, bf16[512,32768]{1,0:T(8,128)(2,1)} %refs_7_.1, bf16[512,32768]{1,0:T(8,128)(2,1)} %refs_7_.1, ...), custom_call_target="tpu_custom_call" | custom-call | tf_op jit(solution)/shard_map/gather_blocks/pallas_call | solution.py:54
  86.0 4.0 %copy-done.2 = bf16[40,512,256]{2,1,0:T(8,128)(2,1)S(1)} copy-done((bf16[40,512,256]{2,1,0:T(8,128)(2,1)S(1)}, bf16[40,512,256]{2,1,0:T(8,128)(2,1)}, u32[]{:S(2)}) %copy-start.2) | copy-done | bytes 10485784
  90.0 1.2 copy-done.4
  91.2 1.3 copy-done.6
  92.5 11.7 %gradient_share.3 = bf16[80,64,128]{2,1,0:T(8,128)(2,1)S(1)} custom-call(s32[40]{0:T(128)S(1)} %get-tuple-element.47.first_ref, s32[40]{0:T(128)S(1)} %get-tuple-element.46.last_ref, s32[40]{0:T(128)S(1)} %convert_reduce_fusion.split_ref, bf16[40,512,256]{2,1,0:T(8,128)(2,1)S(1)} %copy-done.2, bf16[80,64,128]{2,1,0:T(8,128)(2,1)S(1)} %copy-done.6, ...), custom_call_target="tpu_custom_call" | custom-call | tf_op jit(solution)/shard_map/gradient_share/pallas_call | solution.py:99
  104.2 32.1 %code_step0.1 = (bf16[16,320,128]{2,1,0:T(8,128)(2,1)S(1)}, f32[320,128]{1,0:T(8,128)S(1)}, f32[320,128]{1,0:T(8,128)S(1)}) custom-call(bf16[16,320,128]{2,1,0:T(8,128)(2,1)S(1)} %bitcast.54, f32[320,128]{1,0:T(8,128)S(1)} %bitcast_convert_fusion.point_ref.prev_ref, f32[320,128]{1,0:T(8,128)S(1)} %bitcast_convert_fusion.point_ref.prev_ref, ...), custom_call_target="tpu_custom_call" | custom-call | tf_op jit(solution)/shard_map/code_step0/pallas_call | solution.py:273
  136.4 11.7 %gradient_share.4 = bf16[80,64,128]{2,1,0:T(8,128)(2,1)S(1)} custom-call(s32[40]{0:T(128)S(1)} %get-tuple-element.47.first_ref, s32[40]{0:T(128)S(1)} %get-tuple-element.46.last_ref, s32[40]{0:T(128)S(1)} %convert_reduce_fusion.split_ref, bf16[40,512,256]{2,1,0:T(8,128)(2,1)S(1)} %copy-done.3, bf16[80,64,128]{2,1,0:T(8,128)(2,1)S(1)} %bitcast.56, ...), custom_call_target="tpu_custom_call" | custom-call | tf_op jit(solution)/shard_map/gradient_share/pallas_call | solution.py:99
  148.1 31.5 %code_step1.1 = (bf16[16,320,128]{2,1,0:T(8,128)(2,1)S(1)}, f32[320,128]{1,0:T(8,128)S(1)}, f32[320,128]{1,0:T(8,128)S(1)}) custom-call(bf16[16,320,128]{2,1,0:T(8,128)(2,1)S(1)} %bitcast.53, f32[320,128]{1,0:T(8,128)S(1)} %get-tuple-element.16.point_ref, f32[320,128]{1,0:T(8,128)S(1)} %get-tuple-element.17.prev_ref, f32[320,128]{1,0:T(8,128)S(1)} %copy.32.thr_ref), custom_call_target="tpu_custom_call" | custom-call | tf_op jit(solution)/shard_map/code_step1/pallas_call | solution.py:273
  179.6 11.7 %gradient_share.5 = bf16[80,64,128]{2,1,0:T(8,128)(2,1)S(1)} custom-call(s32[40]{0:T(128)S(1)} %get-tuple-element.47.first_ref, s32[40]{0:T(128)S(1)} %get-tuple-element.46.last_ref, s32[40]{0:T(128)S(1)} %convert_reduce_fusion.split_ref, bf16[40,512,256]{2,1,0:T(8,128)(2,1)S(1)} %copy-done.3, bf16[80,64,128]{2,1,0:T(8,128)(2,1)S(1)} %bitcast.55, ...), custom_call_target="tpu_custom_call" | custom-call | tf_op jit(solution)/shard_map/gradient_share/pallas_call | solution.py:99
  191.3 32.1 %code_step2.1 = (bf16[16,320,128]{2,1,0:T(8,128)(2,1)S(1)}, f32[320,128]{1,0:T(8,128)}, f32[320,128]{1,0:T(8,128)}) custom-call(bf16[16,320,128]{2,1,0:T(8,128)(2,1)S(1)} %bitcast.52, f32[320,128]{1,0:T(8,128)S(1)} %get-tuple-element.19.point_ref, f32[320,128]{1,0:T(8,128)S(1)} %get-tuple-element.20.prev_ref, f32[320,128]{1,0:T(8,128)S(1)} %copy.32.thr_ref), custom_call_target="tpu_custom_call" | custom-call | tf_op jit(solution)/shard_map/code_step2/pallas_call | solution.py:273
  223.4 0.6 gather_fusion.2
  224.0 0.1 select_convert_fusion
  224.1 0.1 fusion.9
  224.2 0.0 copy-start.1
  224.3 0.1 dynamic-slice_select_fusion
  224.4 0.9 reshape.312
  225.3 0.0 copy-done.1
  (29 shorter events, 0.3 us)
Async XLA Ops:
  0.0 24.1 %copy-start = (f32[16,64]{1,0:T(8,128)S(1)}, f32[16,64]{1,0:T(8,128)}, u32[]{:S(2)}) copy-start(f32[16,64]{1,0:T(8,128)} %param.15) | copy-start | bytes 12292
  20.2 4.9 %copy-start.10 = (bf16[1,16,4096]{2,1,0:T(8,128)(2,1)S(1)}, bf16[1,16,4096]{2,1,0:T(8,128)(2,1)}, u32[]{:S(2)}) copy-start(bf16[1,16,4096]{2,1,0:T(8,128)(2,1)} %param.11) | copy-start | bytes 393220
  24.1 2.3 %copy-start.9 = (bf16[512,1024]{1,0:T(8,128)(2,1)S(1)}, bf16[512,1024]{1,0:T(8,128)(2,1)}, u32[]{:S(2)}) copy-start(bf16[512,1024]{1,0:T(8,128)(2,1)} %param.10) | copy-start | bytes 3145732
  53.7 3.6 %copy-start.7 = (bf16[16,512,128]{2,1,0:T(8,128)(2,1)S(1)}, bf16[16,512,128]{2,1,0:T(8,128)(2,1)}, u32[]{:S(2)}) copy-start(bf16[16,512,128]{2,1,0:T(8,128)(2,1)} %gather_codes.1) | copy-start | bytes 6291460
  60.6 1.3 copy-start.8
  86.0 4.0 %copy-start.2 = (bf16[40,512,256]{2,1,0:T(8,128)(2,1)S(1)}, bf16[40,512,256]{2,1,0:T(8,128)(2,1)}, u32[]{:S(2)}) copy-start(bf16[40,512,256]{2,1,0:T(8,128)(2,1)} %gather_blocks.1.s_ref) | copy-start | bytes 31457284
  90.0 1.2 copy-start.4
  91.2 1.3 copy-start.6
  92.5 43.9 %copy-start.3 = (bf16[40,512,256]{2,1,0:T(8,128)(2,1)S(1)}, bf16[40,512,256]{2,1,0:T(8,128)(2,1)}, u32[]{:S(2)}) copy-start(bf16[40,512,256]{2,1,0:T(8,128)(2,1)} %gather_blocks.1.s_ref) | copy-start | bytes 31457284
  104.2 32.2 %copy-start.5 = (bf16[1024,512]{1,0:T(8,128)(2,1)S(1)}, bf16[1024,512]{1,0:T(8,128)(2,1)}, u32[]{:S(2)}) copy-start(bf16[1024,512]{1,0:T(8,128)(2,1)} %copy.29) | copy-start | bytes 3145732
  224.2 1.1 copy-start.1

commit v2 on v1

--- a/solution.py
+++ b/solution.py
@@ -31,17 +31,20 @@
 def gather_kernel(ids_ref, *refs):
     out_ref = refs[-1]
     step = pl.program_id(0)
-    lane = lax.broadcasted_iota(jnp.int32, (out_ref.shape[1], 128), 1)
     for pair in range(PER_STEP // 2):
-        sides = []
         for side in range(2):
             slot = 2 * pair + side
+            tile_ref = refs[slot]
+            where_to = pl.ds((pair % 2) * 128 + side * 64, 64)
             half = ids_ref[step * PER_STEP + slot] % 2
-            tile = refs[slot][...].astype(F32)
-            turned = pltpu.roll(tile, 64, 1)
-            sides.append(jnp.where(half == side, tile, turned))
-        both = jnp.where(lane < 64, sides[0], sides[1]).astype(BF16)
-        out_ref[pair // 2, :, pl.ds((pair % 2) * 128, 128)] = both
+
+            @pl.when(half == 0)
+            def _(tile_ref=tile_ref, where_to=where_to, pair=pair):
+                out_ref[pair // 2, :, where_to] = tile_ref[:, :64]
+
+            @pl.when(half == 1)
+            def _(tile_ref=tile_ref, where_to=where_to, pair=pair):
+                out_ref[pair // 2, :, where_to] = tile_ref[:, 64:]
 
 
 def gather_blocks(dictionary, ids):
@@ -78,7 +81,7 @@
         r_ref[last_ref[quad]] += term[PATCHES:]
         return carry
 
-    lax.fori_loop(0, quads, forward, 0, unroll=2)
+    lax.fori_loop(0, quads, forward, 0, unroll=4)
     rb_ref[...] = r_ref[...].astype(BF16)
 
     def backward(quad, carry):
@@ -89,7 +92,7 @@
         out_ref[2 * quad + 1] = g[:, 128:]
         return carry
 
-    lax.fori_loop(0, quads, backward, 0, unroll=2)
+    lax.fori_loop(0, quads, backward, 0, unroll=4)
 
 
 def gradient_share(first, last, split, blocks, z, targets):
@@ -308,18 +311,19 @@
 
     mine = initial_codes.reshape(SLOTS // 2, 2, PATCHES, BLOCK).transpose(0, 2, 1, 3)
     mine = mine.reshape(SLOTS // 2 * PATCHES, 2 * BLOCK)
-    start_all = gather_codes(devices, mine).reshape(groups * SLOTS // 2, PATCHES, 2 * BLOCK)
+    start_all = lax.all_gather(mine, "rows", axis=0).reshape(groups * SLOTS // 2, PATCHES, 2 * BLOCK)
 
     ends = jnp.cumsum(counts)
     starts = ends - counts
     entry = jnp.arange(entries, dtype=jnp.int32)
     group_of = jnp.sum((entry[:, None] >= ends[None, :]).astype(jnp.int32), axis=1)
-    slot_of = entry - jnp.take(starts, group_of)
+    slot_of = entry - jnp.max(jnp.where(entry[:, None] >= starts[None, :], starts[None, :], 0), axis=1)
     ids = jnp.take(support.reshape(-1), group_of * SLOTS + slot_of)
     quads = group_of.reshape(-1, 4)
     first, last = quads[:, 0], quads[:, 3]
     split = jnp.sum((quads == first[:, None]).astype(jnp.int32), axis=1)
-    seat = jnp.argmax(group_order[None, :] == group_of[:, None], axis=1).astype(jnp.int32)
+    seats = jnp.arange(groups, dtype=jnp.int32)[None, :]
+    seat = jnp.sum(jnp.where(group_order[None, :] == group_of[:, None], seats, 0), axis=1)
 
     blocks = gather_blocks(dictionary, ids)
     targets = patches.T.reshape(groups, PATCHES, rows)

time: 227 us -> 197 us (0.87)
  Pallas kernels: 178 us -> 145 us
  between operations: 3.65 us -> 17.2 us
  other arithmetic: 17.9 us -> 5.2 us
  waiting for transfers between devices: 0 us -> 7.99 us
  local copies, waits for them, and re-layouts: 25.6 us -> 20.1 us
    pallas_call x1 -> x0, Pallas kernels: 25.9 us -> none  [gather_codes(): pl.pallas_call(functools.partial(gather_codes_kernel, devices), out_shape...]
    add x1, other arithmetic: 9.94 us -> 0.02 us  [local(): source = (seat * (SLOTS // 2) + slot_of // 2).reshape(pairs, 2)]
    pallas_call x3, Pallas kernels: 35.1 us -> 26.1 us  [gradient_share(): pl.pallas_call(share_kernel, out_shape=jax.ShapeDtypeStruct(z.shape, BF16...]
    all_gather x0 -> x1, waiting for transfers between devices: none -> 7.98 us  [local(): lax.all_gather(mine, 'rows', axis=0)]
    unnamed x22, local copies, waits for them, and re-layouts: 7.36 us -> 1.82 us
    pallas_call x1, Pallas kernels: 21.4 us -> 24.6 us  [gather_blocks(): pl.pallas_call(gather_kernel, out_shape=jax.ShapeDtypeStruct((entries //...]
  transfers between devices with their start and end apart: 0 -> 1, of which waited for: 0 -> 1; matrix products, arithmetic and copies ran while one was open for 0% -> 4% of each run, Pallas kernels for 0% -> 13%
where the time goes in v2:
time: 197 us; the launch traced here: 196 us
  Pallas kernels  145 us (74%)
  local copies, waits for them, and re-layouts  20.1 us (10%)
  between operations  17.2 us (9%)
  waiting for transfers between devices  7.99 us (4%)
  other arithmetic  5.2 us (3%)
    pallas_call x3, Pallas kernels, code_step(): pl.pallas_call(functools.partial(step_kernel, devices, weight), out_shape...  94.7 us
    pallas_call x3, Pallas kernels, gradient_share(): pl.pallas_call(share_kernel, out_shape=jax.ShapeDtypeStruct(z.shape, BF16...  26.1 us
    pallas_call x1, Pallas kernels, gather_blocks(): pl.pallas_call(gather_kernel, out_shape=jax.ShapeDtypeStruct((entries //...  24.6 us
    all_gather x1, waiting for transfers between devices, local(): lax.all_gather(mine, 'rows', axis=0)  7.98 us
    gather x2, local copies, waits for them, and re-layouts, side(): both = jnp.take(start_all, source[:, which], axis=0)  7.12 us
  transfers between devices with their start and end apart: 1, of which 1 were waited for; matrix products, arithmetic and copies ran while one was open for 4% of the time, Pallas kernels for 13%

profile of v2, /device:TPU:0, one launch (start us, length us, event | category | flops | bytes accessed | tf_op | source)
XLA Modules:
  0.0 196.0 jit_solution(5987292596803619412)
XLA Ops:
  6.5 0.0 copy-start
  6.5 0.0 all-gather.2.cloned.1.call-start
  6.6 1.2 reshape.246
  7.8 0.2 copy.49
  8.0 0.0 copy-start.4
  8.0 0.2 all_gather_reshape.3
  8.2 0.8 copy.50
  9.0 0.0 all-gather.2.cloned.1.call-update
  9.0 0.7 dynamic_slice.13
  11.8 0.0 copy-done.6
  11.8 0.7 dynamic-slice.4
  12.4 0.1 copy.46
  12.5 0.1 reduce
  12.7 0.6 dynamic-slice.5
  13.9 0.1 select_reduce_fusion.1
  14.0 0.1 reshape.244
  14.1 0.1 reduce_sum.35
  14.3 0.1 reduce_max.18
  14.4 0.1 reduce_max.17
  15.2 0.1 reshape.245
  15.3 0.1 copy.52
  15.4 0.1 select_reduce_fusion
  15.5 0.1 mul.48
  15.6 0.1 copy.48
  15.7 0.1 copy.47
  15.8 0.7 gather_fusion.1
  16.5 0.1 constant_dynamic-slice_fusion.1
  16.6 0.1 fusion.4
  16.7 0.1 reshape.250
  16.8 0.1 copy.56.thr_ref
  16.9 0.0 copy-done.4
  16.9 1.3 copy.51
  18.2 1.6 gather_fusion
  19.8 0.6 and_select_fusion.1.ids_ref
  20.4 24.6 %gather_blocks.1.s_ref = bf16[40,512,256]{2,1,0:T(8,128)(2,1)} custom-call(s32[160]{0:T(256)} %and_select_fusion.1.ids_ref, bf16[512,32768]{1,0:T(8,128)(2,1)} %refs_7_.1, bf16[512,32768]{1,0:T(8,128)(2,1)} %refs_7_.1, bf16[512,32768]{1,0:T(8,128)(2,1)} %refs_7_.1, bf16[512,32768]{1,0:T(8,128)(2,1)} %refs_7_.1, bf16[512,32768]{1,0:T(8,128)(2,1)} %refs_7_.1, ...), custom_call_target="tpu_custom_call" | custom-call | tf_op jit(solution)/shard_map/gather_blocks/pallas_call | solution.py:57
  45.2 0.2 slice_reduce_fusion.2
  45.4 0.2 slice_reduce_fusion.1
  45.6 0.2 convert_reduce_fusion.split_ref
  45.7 8.0 %all-gather.2.cloned.1.call-done = bf16[16,512,128]{2,1,0:T(8,128)(2,1)} async-done(((bf16[1,512,128]{2,1,0:T(8,128)(2,1)}), bf16[16,512,128]{2,1,0:T(8,128)(2,1)}) %all-gather.2.cloned.1.call-update) | async-done | bytes 2097168 | tf_op jit(solution)/shard_map/all_gather | solution.py:314
  53.7 3.5 %gather_fusion.4 = bf16[80,64,128]{2,1,0:T(8,128)(2,1)} fusion(bf16[128,64,128]{2,1,0:T(8,128)(2,1)} %bitcast.52, s32[1024]{0:T(1024)S(1)} %pad_clamp_fusion.2), kind=kCustom, calls=%fused_computation.1.clone | custom fusion | bytes 2621760 | tf_op jit(solution)/shard_map/jit(_take)/gather | solution.py:335
  57.2 3.6 %gather_fusion.3 = bf16[80,64,128]{2,1,0:T(8,128)(2,1)} fusion(bf16[128,64,128]{2,1,0:T(8,128)(2,1)} %bitcast.53, s32[1024]{0:T(1024)S(1)} %pad_clamp_fusion.3), kind=kCustom, calls=%fused_computation.clone | custom fusion | bytes 2621760 | tf_op jit(solution)/shard_map/jit(_take)/gather | solution.py:335
  60.9 1.6 broadcast_select_fusion.1
  62.5 0.0 slice-start.1
  62.5 0.5 slice_select_fusion.1
  63.0 0.2 broadcast_select_fusion
  63.2 0.0 slice-start.2
  63.2 0.5 slice_select_fusion
  63.7 0.1 fusion
  63.8 0.7 pad_maximum_fusion.z_ref
  64.6 0.1 slice-done.1
  64.7 1.5 slice-done.2
  66.1 0.2 copy-done.2
  66.4 8.7 %gradient_share.3 = bf16[80,64,128]{2,1,0:T(8,128)(2,1)S(1)} custom-call(s32[40]{0:T(128)S(1)} %get-tuple-element.43.first_ref, s32[40]{0:T(128)S(1)} %get-tuple-element.42.last_ref, s32[40]{0:T(128)S(1)} %convert_reduce_fusion.split_ref, bf16[40,512,256]{2,1,0:T(8,128)(2,1)S(1)} %bitcast.42, bf16[80,64,128]{2,1,0:T(8,128)(2,1)S(1)} %pad_maximum_fusion.z_ref, ...), custom_call_target="tpu_custom_call" | custom-call | tf_op jit(solution)/shard_map/gradient_share/pallas_call | solution.py:102
  75.1 29.3 %code_step0.1 = (bf16[16,320,128]{2,1,0:T(8,128)(2,1)S(1)}, f32[320,128]{1,0:T(8,128)S(1)}, f32[320,128]{1,0:T(8,128)S(1)}) custom-call(bf16[16,320,128]{2,1,0:T(8,128)(2,1)S(1)} %bitcast.48, f32[320,128]{1,0:T(8,128)S(1)} %bitcast_convert_fusion.point_ref.prev_ref, f32[320,128]{1,0:T(8,128)S(1)} %bitcast_convert_fusion.point_ref.prev_ref, ...), custom_call_target="tpu_custom_call" | custom-call | tf_op jit(solution)/shard_map/code_step0/pallas_call | solution.py:276
  104.4 8.7 %gradient_share.4 = bf16[80,64,128]{2,1,0:T(8,128)(2,1)S(1)} custom-call(s32[40]{0:T(128)S(1)} %get-tuple-element.43.first_ref, s32[40]{0:T(128)S(1)} %get-tuple-element.42.last_ref, s32[40]{0:T(128)S(1)} %convert_reduce_fusion.split_ref, bf16[40,512,256]{2,1,0:T(8,128)(2,1)S(1)} %bitcast.42, bf16[80,64,128]{2,1,0:T(8,128)(2,1)S(1)} %bitcast.50, ...), custom_call_target="tpu_custom_call" | custom-call | tf_op jit(solution)/shard_map/gradient_share/pallas_call | solution.py:102
  113.1 32.9 %code_step1.1 = (bf16[16,320,128]{2,1,0:T(8,128)(2,1)S(1)}, f32[320,128]{1,0:T(8,128)S(1)}, f32[320,128]{1,0:T(8,128)S(1)}) custom-call(bf16[16,320,128]{2,1,0:T(8,128)(2,1)S(1)} %bitcast.47, f32[320,128]{1,0:T(8,128)S(1)} %get-tuple-element.14.point_ref, f32[320,128]{1,0:T(8,128)S(1)} %get-tuple-element.15.prev_ref, f32[320,128]{1,0:T(8,128)S(1)} %copy.56.thr_ref), custom_call_target="tpu_custom_call" | custom-call | tf_op jit(solution)/shard_map/code_step1/pallas_call | solution.py:276
  146.0 8.7 %gradient_share.5 = bf16[80,64,128]{2,1,0:T(8,128)(2,1)S(1)} custom-call(s32[40]{0:T(128)S(1)} %get-tuple-element.43.first_ref, s32[40]{0:T(128)S(1)} %get-tuple-element.42.last_ref, s32[40]{0:T(128)S(1)} %convert_reduce_fusion.split_ref, bf16[40,512,256]{2,1,0:T(8,128)(2,1)S(1)} %bitcast.42, bf16[80,64,128]{2,1,0:T(8,128)(2,1)S(1)} %bitcast.49, ...), custom_call_target="tpu_custom_call" | custom-call | tf_op jit(solution)/shard_map/gradient_share/pallas_call | solution.py:102
  154.8 32.5 %code_step2.1 = (bf16[16,320,128]{2,1,0:T(8,128)(2,1)S(1)}, f32[320,128]{1,0:T(8,128)}, f32[320,128]{1,0:T(8,128)}) custom-call(bf16[16,320,128]{2,1,0:T(8,128)(2,1)S(1)} %bitcast.46, f32[320,128]{1,0:T(8,128)S(1)} %get-tuple-element.17.point_ref, f32[320,128]{1,0:T(8,128)S(1)} %get-tuple-element.18.prev_ref, f32[320,128]{1,0:T(8,128)S(1)} %copy.56.thr_ref), custom_call_target="tpu_custom_call" | custom-call | tf_op jit(solution)/shard_map/code_step2/pallas_call | solution.py:276
  187.2 0.6 gather_fusion.2
  187.8 0.1 select_convert_fusion
  187.9 0.1 fusion.7
  188.1 0.0 copy-start.1
  188.1 0.1 dynamic-slice_select_fusion
  188.2 0.9 reshape.258
  (33 shorter events, 0.3 us)
Async XLA Ops:
  6.5 9.3 %copy-start = (f32[16,64]{1,0:T(8,128)S(1)}, f32[16,64]{1,0:T(8,128)}, u32[]{:S(2)}) copy-start(f32[16,64]{1,0:T(8,128)} %param.15) | copy-start | bytes 12292
  6.5 2.5 %copy-start.7 = (s32[16]{0:T(128)S(1)}, s32[16]{0:T(128)}, u32[]{:S(2)}) copy-start(s32[16]{0:T(128)} %param.14) | copy-start | bytes 196
  6.5 5.2 %copy-start.6 = (s32[16]{0:T(128)S(1)}, s32[16]{0:T(128)}, u32[]{:S(2)}) copy-start(s32[16]{0:T(128)} %param.13) | copy-start | bytes 196
  6.5 8.7 %copy-start.5 = (s32[16,16]{1,0:T(8,128)S(1)}, s32[16,16]{1,0:T(8,128)}, u32[]{:S(2)}) copy-start(s32[16,16]{1,0:T(8,128)} %param.12) | copy-start | bytes 3076
  6.5 47.2 %all-gather.2.cloned.1.call-start = ((), (), s32[]{:S(2)}) async-start(), calls=%async_computation | async-start | bytes 2228224 | tf_op jit(solution)/shard_map/all_gather | solution.py:314
  8.0 8.9 %copy-start.4 = (bf16[512,1024]{1,0:T(8,128)(2,1)S(1)}, bf16[512,1024]{1,0:T(8,128)(2,1)}, u32[]{:S(2)}) copy-start(bf16[512,1024]{1,0:T(8,128)(2,1)} %param.10) | copy-start | bytes 3145732
  57.2 7.3 %slice-start = ((s8[10485760]{0:T(1024)(128)(4,1)}), s8[2097152]{0:T(1024)(128)(4,1)S(1)}, s32[]{:S(2)}) async-start(s8[10485760]{0:T(1024)(128)(4,1)} %bitcast.41), calls=%async_computation.1 | async-start | bytes 4194304
  60.9 2.1 %copy-start.3 = (bf16[80,64,128]{2,1,0:T(8,128)(2,1)S(1)}, bf16[80,64,128]{2,1,0:T(8,128)(2,1)}, u32[]{:S(2)}) copy-start(bf16[80,64,128]{2,1,0:T(8,128)(2,1)} %gather_fusion.4) | copy-start | bytes 3932164
  62.5 2.2 %slice-start.1 = ((s8[10485760]{0:T(1024)(128)(4,1)}), s8[4194304]{0:T(1024)(128)(4,1)S(1)}, s32[]{:S(2)}) async-start(s8[10485760]{0:T(1024)(128)(4,1)} %bitcast.41), calls=%async_computation.2 | async-start | bytes 8388608
  63.2 2.9 %slice-start.2 = ((s8[10485760]{0:T(1024)(128)(4,1)}), s8[4194304]{0:T(1024)(128)(4,1)S(1)}, s32[]{:S(2)}) async-start(s8[10485760]{0:T(1024)(128)(4,1)} %bitcast.41), calls=%async_computation.3 | async-start | bytes 8388608
  63.8 2.6 %copy-start.2 = (bf16[1024,512]{1,0:T(8,128)(2,1)S(1)}, bf16[1024,512]{1,0:T(8,128)(2,1)}, u32[]{:S(2)}) copy-start(bf16[1024,512]{1,0:T(8,128)(2,1)} %copy.51) | copy-start | bytes 3145732
  188.1 1.1 copy-start.1
Sparse Core Ops, SparseCore 0:
  9.5 44.1 all-gather.1

commit v3 on v2

--- a/solution.py
+++ b/solution.py
@@ -12,7 +12,7 @@
 PATCHES = 64
 ITERS = 3
 LIVE = 10
-PER_STEP = 8
+PER_STEP = 16
 F32 = jnp.float32
 BF16 = jnp.bfloat16
 VMEM = pltpu.VMEM

time: 197 us -> 196 us (level)
  local copies, waits for them, and re-layouts: 20.1 us -> 22.4 us
  transfers between devices with their start and end apart: 1 -> 1, of which waited for: 1 -> 1; matrix products, arithmetic and copies ran while one was open for 4% -> 5% of each run, Pallas kernels for 13% -> 12%
where the time goes in v3:
time: 196 us
  Pallas kernels  144 us (73%)
  local copies, waits for them, and re-layouts  22.4 us (11%)
  between operations  16.7 us (9%)
  waiting for transfers between devices  7.8 us (4%)
  other arithmetic  5.16 us (3%)
    pallas_call x3, Pallas kernels, code_step(): pl.pallas_call(functools.partial(step_kernel, devices, weight), out_shape...  94.5 us
    pallas_call x3, Pallas kernels, gradient_share(): pl.pallas_call(share_kernel, out_shape=jax.ShapeDtypeStruct(z.shape, BF16...  26.1 us
    pallas_call x1, Pallas kernels, gather_blocks(): pl.pallas_call(gather_kernel, out_shape=jax.ShapeDtypeStruct((entries //...  23.1 us
    all_gather x1, waiting for transfers between devices, local(): lax.all_gather(mine, 'rows', axis=0)  7.78 us
    gather x2, local copies, waits for them, and re-layouts, side(): both = jnp.take(start_all, source[:, which], axis=0)  7.1 us
  transfers between devices with their start and end apart: 1, of which 1 were waited for; matrix products, arithmetic and copies ran while one was open for 5% of the time, Pallas kernels for 12%

profile of v3, /device:TPU:0, one launch (start us, length us, event | category | flops | bytes accessed | tf_op | source)
XLA Modules:
  0.0 195.9 jit_solution(4113191406658270291)
XLA Ops:
  6.5 0.0 all-gather.2.cloned.1.call-start
  6.6 1.2 reshape.246
  7.8 0.2 copy.49
  8.0 0.0 copy-start.4
  8.0 0.2 all_gather_reshape.3
  8.2 0.8 copy.50
  9.0 0.0 all-gather.2.cloned.1.call-update
  9.0 0.6 dynamic_slice.13
  11.3 0.6 dynamic-slice.4
  11.8 0.1 copy.46
  12.0 0.1 reduce
  12.1 0.7 dynamic-slice.5
  13.4 0.1 select_reduce_fusion.1
  13.5 0.7 reshape.244
  14.2 0.1 reduce_sum.35
  14.4 0.1 reduce_max.18
  14.5 0.8 reduce_max.17
  15.8 0.0 copy-done.7
  15.8 0.1 reshape.245
  15.9 0.1 copy.52
  16.0 0.1 select_reduce_fusion
  16.1 0.1 mul.48
  16.2 0.7 copy.48
  16.9 0.7 copy.47
  17.6 0.7 gather_fusion.1
  18.3 0.1 constant_dynamic-slice_fusion.1
  18.4 0.1 fusion.4
  18.4 0.1 reshape.250
  18.5 0.1 copy.56.thr_ref
  18.6 0.0 copy-done.4
  18.7 1.3 copy.51
  20.0 1.6 gather_fusion
  21.6 0.5 and_select_fusion.1.ids_ref
  22.2 23.1 %gather_blocks.1.s_ref = bf16[40,512,256]{2,1,0:T(8,128)(2,1)} custom-call(s32[160]{0:T(256)} %and_select_fusion.1.ids_ref, bf16[512,32768]{1,0:T(8,128)(2,1)} %refs_15_.1, bf16[512,32768]{1,0:T(8,128)(2,1)} %refs_15_.1, bf16[512,32768]{1,0:T(8,128)(2,1)} %refs_15_.1, bf16[512,32768]{1,0:T(8,128)(2,1)} %refs_15_.1, bf16[512,32768]{1,0:T(8,128)(2,1)} %refs_15_.1, ...), custom_call_target="tpu_custom_call" | custom-call | tf_op jit(solution)/shard_map/gather_blocks/pallas_call | solution.py:57
  45.4 0.0 copy-done.8
  45.4 0.2 slice_reduce_fusion.2
  45.7 0.2 slice_reduce_fusion.1
  45.9 0.2 convert_reduce_fusion.split_ref
  46.0 7.8 %all-gather.2.cloned.1.call-done = bf16[16,512,128]{2,1,0:T(8,128)(2,1)} async-done(((bf16[1,512,128]{2,1,0:T(8,128)(2,1)}), bf16[16,512,128]{2,1,0:T(8,128)(2,1)}) %all-gather.2.cloned.1.call-update) | async-done | bytes 2097168 | tf_op jit(solution)/shard_map/all_gather | solution.py:314
  53.8 3.5 %gather_fusion.4 = bf16[80,64,128]{2,1,0:T(8,128)(2,1)} fusion(bf16[128,64,128]{2,1,0:T(8,128)(2,1)} %bitcast.52, s32[1024]{0:T(1024)S(1)} %pad_clamp_fusion.2), kind=kCustom, calls=%fused_computation.1.clone | custom fusion | bytes 2621760 | tf_op jit(solution)/shard_map/jit(_take)/gather | solution.py:335
  57.3 3.6 %gather_fusion.3 = bf16[80,64,128]{2,1,0:T(8,128)(2,1)} fusion(bf16[128,64,128]{2,1,0:T(8,128)(2,1)} %bitcast.53, s32[1024]{0:T(1024)S(1)} %pad_clamp_fusion.3), kind=kCustom, calls=%fused_computation.clone | custom fusion | bytes 2621760 | tf_op jit(solution)/shard_map/jit(_take)/gather | solution.py:335
  60.9 1.6 broadcast_select_fusion.1
  62.5 0.0 slice-start.1
  62.5 0.5 slice_select_fusion.1
  63.1 0.2 broadcast_select_fusion
  63.3 0.0 slice-start.2
  63.3 0.5 slice_select_fusion
  63.8 0.1 fusion
  63.9 0.7 pad_maximum_fusion.z_ref
  64.7 0.1 slice-done.1
  64.7 1.5 slice-done.2
  66.2 0.2 copy-done.2
  66.4 8.7 %gradient_share.3 = bf16[80,64,128]{2,1,0:T(8,128)(2,1)S(1)} custom-call(s32[40]{0:T(128)S(1)} %get-tuple-element.43.first_ref, s32[40]{0:T(128)S(1)} %get-tuple-element.42.last_ref, s32[40]{0:T(128)S(1)} %convert_reduce_fusion.split_ref, bf16[40,512,256]{2,1,0:T(8,128)(2,1)S(1)} %bitcast.42, bf16[80,64,128]{2,1,0:T(8,128)(2,1)S(1)} %pad_maximum_fusion.z_ref, ...), custom_call_target="tpu_custom_call" | custom-call | tf_op jit(solution)/shard_map/gradient_share/pallas_call | solution.py:102
  75.1 29.3 %code_step0.1 = (bf16[16,320,128]{2,1,0:T(8,128)(2,1)S(1)}, f32[320,128]{1,0:T(8,128)S(1)}, f32[320,128]{1,0:T(8,128)S(1)}) custom-call(bf16[16,320,128]{2,1,0:T(8,128)(2,1)S(1)} %bitcast.48, f32[320,128]{1,0:T(8,128)S(1)} %bitcast_convert_fusion.point_ref.prev_ref, f32[320,128]{1,0:T(8,128)S(1)} %bitcast_convert_fusion.point_ref.prev_ref, ...), custom_call_target="tpu_custom_call" | custom-call | tf_op jit(solution)/shard_map/code_step0/pallas_call | solution.py:276
  104.4 8.7 %gradient_share.4 = bf16[80,64,128]{2,1,0:T(8,128)(2,1)S(1)} custom-call(s32[40]{0:T(128)S(1)} %get-tuple-element.43.first_ref, s32[40]{0:T(128)S(1)} %get-tuple-element.42.last_ref, s32[40]{0:T(128)S(1)} %convert_reduce_fusion.split_ref, bf16[40,512,256]{2,1,0:T(8,128)(2,1)S(1)} %bitcast.42, bf16[80,64,128]{2,1,0:T(8,128)(2,1)S(1)} %bitcast.50, ...), custom_call_target="tpu_custom_call" | custom-call | tf_op jit(solution)/shard_map/gradient_share/pallas_call | solution.py:102
  113.2 33.0 %code_step1.1 = (bf16[16,320,128]{2,1,0:T(8,128)(2,1)S(1)}, f32[320,128]{1,0:T(8,128)S(1)}, f32[320,128]{1,0:T(8,128)S(1)}) custom-call(bf16[16,320,128]{2,1,0:T(8,128)(2,1)S(1)} %bitcast.47, f32[320,128]{1,0:T(8,128)S(1)} %get-tuple-element.14.point_ref, f32[320,128]{1,0:T(8,128)S(1)} %get-tuple-element.15.prev_ref, f32[320,128]{1,0:T(8,128)S(1)} %copy.56.thr_ref), custom_call_target="tpu_custom_call" | custom-call | tf_op jit(solution)/shard_map/code_step1/pallas_call | solution.py:276
  146.1 8.7 %gradient_share.5 = bf16[80,64,128]{2,1,0:T(8,128)(2,1)S(1)} custom-call(s32[40]{0:T(128)S(1)} %get-tuple-element.43.first_ref, s32[40]{0:T(128)S(1)} %get-tuple-element.42.last_ref, s32[40]{0:T(128)S(1)} %convert_reduce_fusion.split_ref, bf16[40,512,256]{2,1,0:T(8,128)(2,1)S(1)} %bitcast.42, bf16[80,64,128]{2,1,0:T(8,128)(2,1)S(1)} %bitcast.49, ...), custom_call_target="tpu_custom_call" | custom-call | tf_op jit(solution)/shard_map/gradient_share/pallas_call | solution.py:102
  154.9 32.3 %code_step2.1 = (bf16[16,320,128]{2,1,0:T(8,128)(2,1)S(1)}, f32[320,128]{1,0:T(8,128)}, f32[320,128]{1,0:T(8,128)}) custom-call(bf16[16,320,128]{2,1,0:T(8,128)(2,1)S(1)} %bitcast.46, f32[320,128]{1,0:T(8,128)S(1)} %get-tuple-element.17.point_ref, f32[320,128]{1,0:T(8,128)S(1)} %get-tuple-element.18.prev_ref, f32[320,128]{1,0:T(8,128)S(1)} %copy.56.thr_ref), custom_call_target="tpu_custom_call" | custom-call | tf_op jit(solution)/shard_map/code_step2/pallas_call | solution.py:276
  187.1 0.6 gather_fusion.2
  187.7 0.1 select_convert_fusion
  187.8 0.1 fusion.7
  188.0 0.0 copy-start.1
  188.0 0.1 dynamic-slice_select_fusion
  188.1 0.9 reshape.258
  (41 shorter events, 0.3 us)
Async XLA Ops:
  6.5 11.0 %copy-start = (f32[16,64]{1,0:T(8,128)S(1)}, f32[16,64]{1,0:T(8,128)}, u32[]{:S(2)}) copy-start(f32[16,64]{1,0:T(8,128)} %param.15) | copy-start | bytes 12292
  6.5 2.5 %copy-start.11 = (s32[16]{0:T(128)S(1)}, s32[16]{0:T(128)}, u32[]{:S(2)}) copy-start(s32[16]{0:T(128)} %param.14) | copy-start | bytes 196
  6.5 4.7 %copy-start.10 = (s32[16]{0:T(128)S(1)}, s32[16]{0:T(128)}, u32[]{:S(2)}) copy-start(s32[16]{0:T(128)} %param.13) | copy-start | bytes 196
  6.5 9.3 %copy-start.7 = (s32[16,16]{1,0:T(8,128)S(1)}, s32[16,16]{1,0:T(8,128)}, u32[]{:S(2)}) copy-start(s32[16,16]{1,0:T(8,128)} %param.12) | copy-start | bytes 3076
  6.5 47.3 %all-gather.2.cloned.1.call-start = ((), (), s32[]{:S(2)}) async-start(), calls=%async_computation | async-start | bytes 2228224 | tf_op jit(solution)/shard_map/all_gather | solution.py:314
  8.0 10.7 %copy-start.4 = (bf16[512,1024]{1,0:T(8,128)(2,1)S(1)}, bf16[512,1024]{1,0:T(8,128)(2,1)}, u32[]{:S(2)}) copy-start(bf16[512,1024]{1,0:T(8,128)(2,1)} %param.10) | copy-start | bytes 3145732
  22.1 23.2 %copy-start.8 = (s32[80,2]{0,1:T(2,128)S(1)}, s32[80,2]{0,1:T(2,128)}, u32[]{:S(2)}) copy-start(s32[80,2]{0,1:T(2,128)} %copy.48) | copy-start | bytes 1924
  22.2 23.2 %copy-start.9 = (s32[80,2]{0,1:T(2,128)S(1)}, s32[80,2]{0,1:T(2,128)}, u32[]{:S(2)}) copy-start(s32[80,2]{0,1:T(2,128)} %copy.47) | copy-start | bytes 1924
  22.2 23.3 %copy-start.5 = (s32[40,4]{1,0:T(8,128)S(1)}, s32[40,4]{1,0:T(8,128)}, u32[]{:S(2)}) copy-start(s32[40,4]{1,0:T(8,128)} %reshape.244) | copy-start | bytes 1924
  22.2 23.5 %copy-start.6 = (s32[80,2,1,1]{1,0,3,2:T(8,128)S(1)}, s32[80,2,1,1]{1,0,3,2:T(8,128)}, u32[]{:S(2)}) copy-start(s32[80,2,1,1]{1,0,3,2:T(8,128)} %reduce_max.17) | copy-start | bytes 1924
  57.3 7.3 %slice-start = ((s8[10485760]{0:T(1024)(128)(4,1)}), s8[2097152]{0:T(1024)(128)(4,1)S(1)}, s32[]{:S(2)}) async-start(s8[10485760]{0:T(1024)(128)(4,1)} %bitcast.41), calls=%async_computation.1 | async-start | bytes 4194304
  60.9 2.1 %copy-start.3 = (bf16[80,64,128]{2,1,0:T(8,128)(2,1)S(1)}, bf16[80,64,128]{2,1,0:T(8,128)(2,1)}, u32[]{:S(2)}) copy-start(bf16[80,64,128]{2,1,0:T(8,128)(2,1)} %gather_fusion.4) | copy-start | bytes 3932164
  62.5 2.2 %slice-start.1 = ((s8[10485760]{0:T(1024)(128)(4,1)}), s8[4194304]{0:T(1024)(128)(4,1)S(1)}, s32[]{:S(2)}) async-start(s8[10485760]{0:T(1024)(128)(4,1)} %bitcast.41), calls=%async_computation.2 | async-start | bytes 8388608
  63.3 2.9 %slice-start.2 = ((s8[10485760]{0:T(1024)(128)(4,1)}), s8[4194304]{0:T(1024)(128)(4,1)S(1)}, s32[]{:S(2)}) async-start(s8[10485760]{0:T(1024)(128)(4,1)} %bitcast.41), calls=%async_computation.3 | async-start | bytes 8388608
  63.9 2.6 %copy-start.2 = (bf16[1024,512]{1,0:T(8,128)(2,1)S(1)}, bf16[1024,512]{1,0:T(8,128)(2,1)}, u32[]{:S(2)}) copy-start(bf16[1024,512]{1,0:T(8,128)(2,1)} %copy.51) | copy-start | bytes 3145732
  188.0 1.1 copy-start.1
Sparse Core Ops, SparseCore 0:
  9.5 44.2 all-gather.1
